TPU v7x, 32 devices: a whole 2x2x4 slice. The times are simulated.
32 devices in a mesh: parts: 2 (over x), wide: 16 (over z, y, core).
Axes of the slice: x: 2, y: 2, z: 4, core: 2. Of those that a mesh axis runs over, the one named last changes fastest.
Arguments:
- voxels: bfloat16 [32768, 256], P(('parts', 'wide')), parts along dimension 0, may hold values from -16 to 16
- regular_window: int32 [32768], P(('parts', 'wide')), parts along dimension 0, may hold values from 0 to 127, never falling along the last dimension, each value on 1 to 256 neighbouring positions
- shifted_window: int32 [32768], P(('parts', 'wide')), parts along dimension 0, may hold values from 0 to 127, never falling along the last dimension, each value on 1 to 256 neighbouring positions
- dest: int32 [32768], P(('parts', 'wide')), parts along dimension 0, may hold values from 0 to 16383, as said below
- w_qkv: bfloat16 [2, 256, 768], replicated, may hold values from -0.375 to 0.375
- w_out: bfloat16 [2, 256, 256], replicated, may hold values from -1.5 to 1.5
- gain: float32 [2, 256], replicated, may hold values from 0.1 to 1.9
- temper: float32 [2, 8], replicated, may hold values from 0.5 to 6
Outputs:
- shifted_out: bfloat16 [32768, 256], P(('parts', 'wide')), parts along dimension 0
There are 2 independent parts, one for each index of `parts`. A program takes and returns all parts, laid end to end along the dimension named above; an argument that names none is the same for every part. Nothing has to cross between parts.
Inputs may be any that keep to these rules, and one draw needn't show every extreme that they name: `regular_window`: window ids never fall along the order; every window has 1 to 256 voxels and one has exactly 256. `shifted_window`: window ids never fall along the order; every window has 1 to 256 voxels and one has exactly 256. dest is a permutation. Counting blocks of 1024 consecutive positions, at most 128 voxels go from one block of the regular order to one block of the shifted order, and some pair reaches 128; the count from a block to the block k places further along, cyclically, is the same for every block.
All inputs are finite; a program needn't handle non-finite values.
Results may differ from a plain program's by a relative error of at most 0.007.
The roundings to bfloat16 on the way count: a program that leaves them out, or rounds other values in their place, can miss the bound.
Values may be sent and summed in bfloat16 or wider, within the bound.
A program may use at most 64 MiB of HBM per device.

v0:
```python
import math
import jax
import jax.numpy as jnp
from jax import lax
from jax.sharding import PartitionSpec as P

HEADS = 8
epsilon = 1e-05
masked_score = -1e30


def extended(block, sides, width):
    for axis, dim in sides:
        count = lax.axis_size(axis)
        forward = [(i, i + 1) for i in range(count - 1)]
        backward = [(target, source) for source, target in forward]
        low = lax.ppermute(
            lax.slice_in_dim(block, block.shape[dim] - width, None, axis=dim), axis, forward
        )
        high = lax.ppermute(lax.slice_in_dim(block, 0, width, axis=dim), axis, backward)
        block = jnp.concatenate([low, block, high], axis=dim)
    return block


def settle(hidden, attended, w_out_layer, gain_layer):
    summed = hidden.astype(jnp.float32) + jnp.dot(
        attended, w_out_layer, preferred_element_type=jnp.float32
    )
    center = jnp.mean(summed, axis=1, keepdims=True)
    spread = jnp.mean(jnp.square(summed - center), axis=1, keepdims=True)
    return ((summed - center) * lax.rsqrt(spread + epsilon) * gain_layer).astype(jnp.bfloat16)


def window_attention(queries, padded, marks_own, marks_pad, factor, rim_width):
    total_rows = queries.shape[0]
    channels = queries.shape[1]
    head_dim = channels // HEADS
    block_rows = min(512, total_rows)
    key_rows = block_rows + 2 * rim_width
    results = []
    for number in range(total_rows // block_rows):
        first_row = number * block_rows
        query_block = queries[first_row : first_row + block_rows]
        key_block = padded[first_row : first_row + key_rows]
        mark_query = marks_own[first_row : first_row + block_rows]
        mark_key = marks_pad[first_row : first_row + key_rows]
        same_window = mark_query[:, None] == mark_key[None, :]

        def per_head(
            head_index, query_block=query_block, key_block=key_block, same_window=same_window
        ):
            query_part = lax.dynamic_slice_in_dim(query_block, head_index * head_dim, head_dim, 1)
            keys_part = lax.dynamic_slice_in_dim(key_block, head_index * head_dim, head_dim, 1)
            values_part = lax.dynamic_slice_in_dim(
                key_block, channels + head_index * head_dim, head_dim, 1
            )
            scores = lax.dot_general(
                query_part, keys_part, (((1,), (1,)), ((), ())), preferred_element_type=jnp.float32
            )
            scores = scores * factor[head_index]
            scores = jnp.where(same_window, scores, masked_score)
            highest = jnp.max(scores, axis=1, keepdims=True)
            exponents = jnp.where(same_window, jnp.exp(scores - highest), 0.0)
            totals = jnp.sum(exponents, axis=1, keepdims=True)
            weights = (exponents / totals).astype(jnp.bfloat16)
            return jnp.dot(weights, values_part, preferred_element_type=jnp.float32).astype(
                jnp.bfloat16
            )

        heads_out = lax.map(per_head, jnp.arange(HEADS, dtype=jnp.int32))
        results.append(jnp.transpose(heads_out, (1, 0, 2)).reshape(block_rows, channels))
    return jnp.concatenate(results, axis=0)


def sublayer(hidden, window_ids, w_qkv_layer, w_out_layer, gain_layer, temper_layer):
    local_rows = hidden.shape[0]
    channels = hidden.shape[1]
    rim_width = local_rows // 4
    marks = window_ids + 1
    factor = temper_layer * (1.0 / math.sqrt(channels // HEADS))
    projected = jnp.dot(hidden, w_qkv_layer, preferred_element_type=jnp.float32).astype(
        jnp.bfloat16
    )
    key_vals = projected[:, channels:]
    padded, marks_pad = (
        extended(key_vals, (("wide", 0),), rim_width),
        extended(marks, (("wide", 0),), rim_width),
    )
    queries = projected[:, :channels]
    attended = window_attention(queries, padded, marks, marks_pad, factor, rim_width)
    return settle(hidden, attended, w_out_layer, gain_layer)


def regroup_rows(first, dest):
    local_rows = first.shape[0]
    channels = first.shape[1]
    devices = lax.axis_size("wide")
    capacity = 2 * local_rows // devices
    target = dest // local_rows
    slot_within = dest - target * local_rows
    matches = (target[:, None] == jnp.arange(devices, dtype=jnp.int32)[None, :]).astype(jnp.int32)
    position = jnp.sum(jnp.cumsum(matches, axis=0) * matches, axis=1) - 1
    buffer_row = target * capacity + position
    outgoing = jnp.zeros((devices * capacity, channels), jnp.bfloat16).at[buffer_row].set(first)
    slot_list = (
        jnp.full((devices * capacity,), local_rows, jnp.int32).at[buffer_row].set(slot_within)
    )
    arrived, arrived_slots = (
        lax.all_to_all(outgoing, "wide", split_axis=0, concat_axis=0, tiled=True),
        lax.all_to_all(slot_list, "wide", split_axis=0, concat_axis=0, tiled=True),
    )
    return (
        jnp.zeros((local_rows, channels), jnp.bfloat16).at[arrived_slots].set(arrived, mode="drop")
    )


def body(voxels, regular_window, shifted_window, dest, w_qkv, w_out, gain, temper):
    first = sublayer(voxels, regular_window, w_qkv[0], w_out[0], gain[0], temper[0])
    moved = regroup_rows(first, dest)
    return sublayer(moved, shifted_window, w_qkv[1], w_out[1], gain[1], temper[1])


def solution(mesh):
    in_specs = (
        P(("parts", "wide"), None),
        P(("parts", "wide")),
        P(("parts", "wide")),
        P(("parts", "wide")),
        P(),
        P(),
        P(),
        P(),
    )
    out_specs = P(("parts", "wide"), None)
    return jax.shard_map(body, mesh=mesh, in_specs=in_specs, out_specs=out_specs, check_vma=False)
```

profile of v0, /device:TPU:13, one launch (start us, length us, event | category | flops | bytes accessed | tf_op | source)
XLA Modules:
  0.0 406.4 jit_solution(13931724288074019573)
XLA Ops:
  2.6 3.8 collective-permute-start
  8.4 4.5 %collective-permute-start.1 = (s32[256]{0:T(256)S(1)}, s32[256]{0:T(256)S(1)}, u32[]{:S(2)}, u32[]{:S(2)}) collective-permute-start(s32[256]{0:T(256)S(1)} %get-tuple-element.539), channel_id=1, source_target_pairs={{0,1},{1,2},{2,3},{3,4},{4,5},{5,6},{6,7},{7,8},{8,9},{9,10},{10,1... | collective-permute-start | bytes 3080 | tf_op jit(solution)/shard_map/ppermute | solution.py:17
  14.9 4.5 %reduce-window.6 = s32[16,8,128]{2,1,0:T(8,128)S(1)} reduce-window(s32[16,8,128]{2,1,0:T(8,128)S(1)} %fusion.76, s32[]{:T(128)} %constant.259.clone.1), window={size=1x1x128 pad=0_0x0_0x127_0}, to_apply=%region_0.1 | reduce-window | flops 2080768 | bytes 131076 | tf_op jit(solution)/shard_map/reduce-window
  19.9 4.9 %scatter_custom_fusion = s32[2048]{0:T(1024)} fusion(s32[1024]{0:T(1024)S(1)} %get-tuple-element.542, s32[1024]{0:T(1024)S(1)} %get-tuple-element.541, s32[]{:T(128)} %constant.257.clone.1), kind=kCustom, calls=%fused_computation.123 | custom fusion | bytes 8196 | tf_op jit(solution)/shard_map/scatter | solution.py:106
  24.8 6.4 %all-to-all-start = ((s32[16,128,1]{1,2,0:T(1,128)}), s32[16,128,1]{1,2,0:T(1,128)S(1)}, u32[]{:S(2)}, u32[]{:S(2)}) async-start(s32[16,128,1]{1,2,0:T(1,128)} %bitcast.4), calls=%async_computation | async-start | bytes 16384 | tf_op jit(solution)/shard_map/all_to_all | solution.py:110
  33.2 2.5 pad_maximum_fusion.3
  35.7 78.1 %while.52 = (s32[]{:T(128)}, bf16[8,512,32]{1,2,0:T(8,128)(2,1)S(1)}, s32[8]{0:T(128)S(1)}, bf16[512,256]{1,0:T(8,128)(2,1)}, bf16[1024,512]{1,0:T(8,128)(2,1)},...) while((s32[]{:T(128)}, ...), condition=%wide.region_7.8_spmd.clone, body=%wide.region_4.7_spmd.clone.sunk | while | flops 76037128 | bytes 7010112 | solution.py:70
  39.4 2.2 fusion.114
  43.0 2.5 fusion.116
  49.2 2.3 fusion.114
  52.7 2.5 fusion.116
  58.9 2.2 fusion.114
  62.5 2.5 fusion.116
  68.7 2.3 fusion.114
  72.2 2.5 fusion.116
  82.0 2.5 fusion.116
  88.2 2.3 fusion.114
  91.8 2.5 fusion.116
  101.5 2.5 fusion.116
  107.7 2.3 fusion.114
  111.3 2.5 fusion.116
  113.9 74.5 %while.53 = (s32[]{:T(128)}, bf16[8,512,32]{1,2,0:T(8,128)(2,1)S(1)}, s32[8]{0:T(128)S(1)}, bf16[512,256]{1,0:T(8,128)(2,1)}, bf16[1024,512]{1,0:T(8,128)(2,1)},...) while((s32[]{:T(128)}, ...), condition=%wide.region_11.12_spmd.clone, body=%wide.region_8.11_spmd.clone.sunk | while | flops 76037128 | bytes 7010112 | solution.py:70
  120.7 2.4 fusion.120
  130.0 2.4 fusion.120
  139.4 2.4 fusion.120
  148.7 2.4 fusion.120
  158.0 2.4 fusion.120
  167.3 2.4 fusion.120
  176.6 2.4 fusion.120
  185.9 2.4 fusion.120
  189.3 6.0 %scatter_custom_fusion.1 = bf16[2048,256]{1,0:T(8,128)(2,1)} fusion(s32[1024]{0:T(1024)S(1)} %get-tuple-element.542, bf16[1024,256]{1,0:T(8,128)(2,1)S(1)} %copy.23, bf16[]{:T(256)} %constant.256.clone.1), kind=kCustom, calls=%fused_computation.89 | custom fusion | bytes 1048578 | tf_op jit(solution)/shard_map/scatter | solution.py:104
  195.3 6.0 %all-to-all-start.1 = ((bf16[16,128,256]{2,1,0:T(8,128)(2,1)}), bf16[16,128,256]{2,1,0:T(8,128)(2,1)S(1)}, u32[]{:S(2)}, u32[]{:S(2)}) async-start(bf16[16,128,256]{2,1,0:T(8,128)(2,1)} %bitcast.15), calls=%async_computation.1 | async-start | bytes 2097152 | tf_op jit(solution)/shard_map/all_to_all | solution.py:109
  201.4 3.4 collective-permute-start.5
  206.9 19.3 %all-to-all-done.1 = bf16[16,128,256]{2,1,0:T(8,128)(2,1)S(1)} async-done(((bf16[16,128,256]{2,1,0:T(8,128)(2,1)}), bf16[16,128,256]{2,1,0:T(8,128)(2,1)S(1)}, u32[]{:S(2)}, u32[]{:S(2)}) %all-to-all-start.1) | async-done | bytes 1048608 | tf_op jit(solution)/shard_map/all_to_all | solution.py:109
  226.2 9.4 %scatter_custom_fusion.2 = bf16[1024,256]{1,0:T(8,128)(2,1)S(1)} fusion(s32[2048]{0:T(1024)S(1)} %bitcast.115, bf16[2048,256]{1,0:T(8,128)(2,1)S(1)} %bitcast.112, bf16[]{:T(256)} %constant.256.clone.1), kind=kCustom, calls=%fused_computation.95 | custom fusion | bytes 524290 | tf_op jit(solution)/shard_map/scatter | solution.py:113
  237.0 3.7 collective-permute-start.4
  244.5 5.0 %collective-permute-done.6 = bf16[256,512]{1,0:T(8,128)(2,1)} collective-permute-done((bf16[256,512]{1,0:T(8,128)(2,1)}, bf16[256,512]{1,0:T(8,128)(2,1)}, u32[]{:S(2)}, u32[]{:S(2)}) %collective-permute-start.6) | collective-permute-done | bytes 262176 | tf_op jit(solution)/shard_map/ppermute | solution.py:20
  249.6 2.5 pad_maximum_fusion.1
  252.1 78.1 %while.54 = (s32[]{:T(128)}, bf16[8,512,32]{1,2,0:T(8,128)(2,1)S(1)}, s32[8]{0:T(128)S(1)}, bf16[512,256]{1,0:T(8,128)(2,1)}, bf16[1024,512]{1,0:T(8,128)(2,1)},...) while((s32[]{:T(128)}, ...), condition=%wide.region_19.20_spmd.clone, body=%wide.region_16.19_spmd.clone.sunk | while | flops 76037128 | bytes 7010112 | solution.py:70
  255.7 2.2 fusion.122
  259.3 2.5 fusion.124
  265.5 2.2 fusion.122
  269.1 2.5 fusion.124
  275.3 2.2 fusion.122
  278.8 2.5 fusion.124
  285.0 2.2 fusion.122
  288.6 2.5 fusion.124
  294.8 2.2 fusion.122
  298.3 2.5 fusion.124
  304.5 2.2 fusion.122
  308.1 2.5 fusion.124
  314.3 2.2 fusion.122
  317.9 2.5 fusion.124
  324.1 2.2 fusion.122
  327.6 2.5 fusion.124
  330.2 74.5 %while.55 = (s32[]{:T(128)}, bf16[8,512,32]{1,2,0:T(8,128)(2,1)S(1)}, s32[8]{0:T(128)S(1)}, bf16[512,256]{1,0:T(8,128)(2,1)}, bf16[1024,512]{1,0:T(8,128)(2,1)},...) while((s32[]{:T(128)}, ...), condition=%wide.region_23.24_spmd.clone, body=%wide.region_20.23_spmd.clone.sunk | while | flops 76037128 | bytes 7010112 | solution.py:70
  337.1 2.4 fusion.128
  346.4 2.4 fusion.128
  355.7 2.4 fusion.128
  365.0 2.4 fusion.128
  374.3 2.4 fusion.128
  383.6 2.4 fusion.128
  392.9 2.4 fusion.128
  402.3 2.4 fusion.128
  (199 shorter events, 136.5 us)
Async XLA Ops:
  0.0 8.4 %copy-start.7 = (s32[1024]{0:T(1024)S(1)}, s32[1024]{0:T(1024)}, u32[]{:S(2)}) copy-start(s32[1024]{0:T(1024)} %param.17) | copy-start | bytes 12292
  0.0 14.9 %copy-start.6 = (s32[1024]{0:T(1024)S(1)}, s32[1024]{0:T(1024)}, u32[]{:S(2)}) copy-start(s32[1024]{0:T(1024)} %param.19) | copy-start | bytes 12292
  0.0 32.0 %copy-start.9 = (f32[2,256]{1,0:T(2,128)S(1)}, f32[2,256]{1,0:T(2,128)}, u32[]{:S(2)}) copy-start(f32[2,256]{1,0:T(2,128)} %param.22) | copy-start | bytes 6148
  0.0 32.0 %copy-start.10 = (f32[2,8]{1,0:T(2,128)S(1)}, f32[2,8]{1,0:T(2,128)}, u32[]{:S(2)}) copy-start(f32[2,8]{1,0:T(2,128)} %param.23) | copy-start | bytes 196
  2.6 29.5 %copy-start = (bf16[1024,256]{1,0:T(8,128)(2,1)S(1)}, bf16[1024,256]{1,0:T(8,128)(2,1)}, u32[]{:S(2)}) copy-start(bf16[1024,256]{1,0:T(8,128)(2,1)} %param.16) | copy-start | bytes 1572868
  2.6 30.6 %collective-permute-start = (bf16[256,512]{1,0:T(8,128)(2,1)}, bf16[256,512]{1,0:T(8,128)(2,1)S(1)}, u32[]{:S(2)}, u32[]{:S(2)}) collective-permute-start(bf16[256,512]{1,0:T(8,128)(2,1)} %get-tuple-element.521), channel_id=1, source_target_pairs={{0,1},{1,2},{2,3},{3,4},{4,5},{5,6},{6,7},{7,8},{8,9},{9,10},{10,1... | collective-permute-start | bytes 786440 | tf_op jit(solution)/shard_map/ppermute | solution.py:17
  6.5 26.7 %collective-permute-start.2 = (bf16[256,512]{1,0:T(8,128)(2,1)}, bf16[256,512]{1,0:T(8,128)(2,1)}, u32[]{:S(2)}, u32[]{:S(2)}) collective-permute-start(bf16[256,512]{1,0:T(8,128)(2,1)} %get-tuple-element.522), channel_id=1, source_target_pairs={{1,0},{2,1},{3,2},{4,3},{5,4},{6,5},{7,6},{8,7},{9,8},{10,9},{11,1... | collective-permute-start | bytes 786440 | tf_op jit(solution)/shard_map/ppermute | solution.py:20
  8.4 24.8 %collective-permute-start.1 = (s32[256]{0:T(256)S(1)}, s32[256]{0:T(256)S(1)}, u32[]{:S(2)}, u32[]{:S(2)}) collective-permute-start(s32[256]{0:T(256)S(1)} %get-tuple-element.539), channel_id=1, source_target_pairs={{0,1},{1,2},{2,3},{3,4},{4,5},{5,6},{6,7},{7,8},{8,9},{9,10},{10,1... | collective-permute-start | bytes 3080 | tf_op jit(solution)/shard_map/ppermute | solution.py:17
  13.0 20.2 %collective-permute-start.3 = (s32[256]{0:T(256)S(1)}, s32[256]{0:T(256)S(1)}, u32[]{:S(2)}, u32[]{:S(2)}) collective-permute-start(s32[256]{0:T(256)S(1)} %get-tuple-element.540), channel_id=1, source_target_pairs={{1,0},{2,1},{3,2},{4,3},{5,4},{6,5},{7,6},{8,7},{9,8},{10,9},{11,1... | collective-permute-start | bytes 3080 | tf_op jit(solution)/shard_map/ppermute | solution.py:20
  24.8 170.5 %all-to-all-start = ((s32[16,128,1]{1,2,0:T(1,128)}), s32[16,128,1]{1,2,0:T(1,128)S(1)}, u32[]{:S(2)}, u32[]{:S(2)}) async-start(s32[16,128,1]{1,2,0:T(1,128)} %bitcast.4), calls=%async_computation | async-start | bytes 16384 | tf_op jit(solution)/shard_map/all_to_all | solution.py:110
  113.8 74.5 %copy-start.1 = (bf16[1024,256]{0,1:T(8,128)(2,1)S(1)}, bf16[1024,256]{0,1:T(8,128)(2,1)}, u32[]{:S(2)}) copy-start(bf16[1024,256]{0,1:T(8,128)(2,1)} %copy.22) | copy-start | bytes 1572868
  113.9 74.5 %copy-start.4 = (bf16[2,256,256]{2,1,0:T(8,128)(2,1)S(1)}, bf16[2,256,256]{2,1,0:T(8,128)(2,1)}, u32[]{:S(2)}) copy-start(bf16[2,256,256]{2,1,0:T(8,128)(2,1)} %param.21) | copy-start | bytes 786436
  189.1 12.3 %copy-start.8 = (s32[1024]{0:T(1024)S(1)}, s32[1024]{0:T(1024)}, u32[]{:S(2)}) copy-start(s32[1024]{0:T(1024)} %param.18) | copy-start | bytes 12292
  189.3 46.3 %copy-start.3 = (bf16[2,256,768]{2,1,0:T(8,128)(2,1)S(1)}, bf16[2,256,768]{2,1,0:T(8,128)(2,1)}, u32[]{:S(2)}) copy-start(bf16[2,256,768]{2,1,0:T(8,128)(2,1)} %param.20) | copy-start | bytes 2359300
  195.3 30.9 %all-to-all-start.1 = ((bf16[16,128,256]{2,1,0:T(8,128)(2,1)}), bf16[16,128,256]{2,1,0:T(8,128)(2,1)S(1)}, u32[]{:S(2)}, u32[]{:S(2)}) async-start(bf16[16,128,256]{2,1,0:T(8,128)(2,1)} %bitcast.15), calls=%async_computation.1 | async-start | bytes 2097152 | tf_op jit(solution)/shard_map/all_to_all | solution.py:109
  201.4 41.2 %collective-permute-start.5 = (s32[256]{0:T(256)S(1)}, s32[256]{0:T(256)S(1)}, u32[]{:S(2)}, u32[]{:S(2)}) collective-permute-start(s32[256]{0:T(256)S(1)} %get-tuple-element.533), channel_id=1, source_target_pairs={{0,1},{1,2},{2,3},{3,4},{4,5},{5,6},{6,7},{7,8},{8,9},{9,10},{10,1... | collective-permute-start | bytes 3080 | tf_op jit(solution)/shard_map/ppermute | solution.py:17
  204.8 37.8 %collective-permute-start.7 = (s32[256]{0:T(256)S(1)}, s32[256]{0:T(256)S(1)}, u32[]{:S(2)}, u32[]{:S(2)}) collective-permute-start(s32[256]{0:T(256)S(1)} %get-tuple-element.534), channel_id=1, source_target_pairs={{1,0},{2,1},{3,2},{4,3},{5,4},{6,5},{7,6},{8,7},{9,8},{10,9},{11,1... | collective-permute-start | bytes 3080 | tf_op jit(solution)/shard_map/ppermute | solution.py:20
  237.0 7.6 %collective-permute-start.4 = (bf16[256,512]{1,0:T(8,128)(2,1)}, bf16[256,512]{1,0:T(8,128)(2,1)S(1)}, u32[]{:S(2)}, u32[]{:S(2)}) collective-permute-start(bf16[256,512]{1,0:T(8,128)(2,1)} %get-tuple-element.517), channel_id=1, source_target_pairs={{0,1},{1,2},{2,3},{3,4},{4,5},{5,6},{6,7},{7,8},{8,9},{9,10},{10,1... | collective-permute-start | bytes 786440 | tf_op jit(solution)/shard_map/ppermute | solution.py:17
  240.6 8.9 %collective-permute-start.6 = (bf16[256,512]{1,0:T(8,128)(2,1)}, bf16[256,512]{1,0:T(8,128)(2,1)}, u32[]{:S(2)}, u32[]{:S(2)}) collective-permute-start(bf16[256,512]{1,0:T(8,128)(2,1)} %get-tuple-element.518), channel_id=1, source_target_pairs={{1,0},{2,1},{3,2},{4,3},{5,4},{6,5},{7,6},{8,7},{9,8},{10,9},{11,1... | collective-permute-start | bytes 786440 | tf_op jit(solution)/shard_map/ppermute | solution.py:20
  330.2 74.5 %copy-start.2 = (bf16[1024,256]{0,1:T(8,128)(2,1)S(1)}, bf16[1024,256]{0,1:T(8,128)(2,1)}, u32[]{:S(2)}) copy-start(bf16[1024,256]{0,1:T(8,128)(2,1)} %copy.24) | copy-start | bytes 1572868
  330.2 74.5 %copy-start.5 = (bf16[2,256,256]{2,1,0:T(8,128)(2,1)S(1)}, bf16[2,256,256]{2,1,0:T(8,128)(2,1)}, u32[]{:S(2)}) copy-start(bf16[2,256,256]{2,1,0:T(8,128)(2,1)} %param.21) | copy-start | bytes 786436
where the time goes:
time: 410 us; the launch traced here: 406 us
  matrix products  153 us (37%)
  loops' own time  76.8 us (19%)
  local copies, waits for them, and re-layouts  65 us (16%)
  other arithmetic  50.9 us (12%)
  starting transfers between devices  35.7 us (9%)
  waiting for transfers between devices  24.3 us (6%)
    dot_general x32, matrix products, per_head(): jnp.dot(weights, values_part, preferred_element_type=jnp.float32)  79.2 us
    another operation x4, loops' own time, window_attention(): heads_out = lax.map(per_head, jnp.arange(HEADS, dtype=jnp.int32))  76.8 us
    dot_general x32, matrix products, per_head(): lax.dot_general(query_part, keys_part, (((1,), (1,)), ((), ())), preferre...  71 us
    reduce_sum x32, other arithmetic, per_head(): totals = jnp.sum(exponents, axis=1, keepdims=True)  40.6 us
    all_to_all x1, waiting for transfers between devices, regroup_rows(): lax.all_to_all(outgoing, 'wide', split_axis=0, concat_axis=0, tiled=True)  19.3 us
    dynamic_slice x32, local copies, waits for them, and re-layouts, window_attention(): heads_out = lax.map(per_head, jnp.arange(HEADS, dtype=jnp.int32))  18.8 us
    dynamic_slice x32, local copies, waits for them, and re-layouts, per_head(): scores = scores * factor[head_index]  18.8 us
    ppermute x4, starting transfers between devices, extended(): lax.ppermute(lax.slice_in_dim(block, block.shape[dim] - width, None, axis...  15.4 us
  transfers between devices with their start and end apart: 10, of which 2 were waited for; matrix products, arithmetic and copies ran while one was open for 36% of the time, Pallas kernels for 0%

commit v1 on v0

--- a/solution.py
+++ b/solution.py
@@ -7,6 +7,22 @@
 HEADS = 8
 epsilon = 1e-05
 masked_score = -1e30
+
+
+def exchange_in_pairs(shard, axis, split, join):
+    ways, here = (lax.axis_size(axis), lax.axis_index(axis))
+    width = shard.shape[split] // ways
+    lengths = list(shard.shape)
+    lengths[split] = width
+    height = lengths[join]
+    lengths[join] = height * ways
+    full = jnp.zeros(lengths, shard.dtype)
+    for mask in range(ways):
+        part = lax.dynamic_slice_in_dim(shard, (here ^ mask) * width, width, axis=split)
+        if mask:
+            part = lax.ppermute(part, axis, [(d, d ^ mask) for d in range(ways)])
+        full = lax.dynamic_update_slice_in_dim(full, part, (here ^ mask) * height, axis=join)
+    return full
 
 
 def extended(block, sides, width):
@@ -106,7 +122,7 @@
         jnp.full((devices * capacity,), local_rows, jnp.int32).at[buffer_row].set(slot_within)
     )
     arrived, arrived_slots = (
-        lax.all_to_all(outgoing, "wide", split_axis=0, concat_axis=0, tiled=True),
+        exchange_in_pairs(outgoing, "wide", 0, 0),
         lax.all_to_all(slot_list, "wide", split_axis=0, concat_axis=0, tiled=True),
     )
     return (

time: 410 us -> 431 us (1.051)
  starting transfers between devices: 35.7 us -> 51.2 us
  waiting for transfers between devices: 24.3 us -> 18.3 us
    ppermute x0 -> x15, starting transfers between devices: none -> 21.4 us  [exchange_in_pairs(): part = lax.ppermute(part, axis, [(d, d ^ mask) for d in range(ways)])]
    all_to_all x1 -> x0, waiting for transfers between devices: 19.3 us -> none  [regroup_rows(): lax.all_to_all(outgoing, 'wide', split_axis=0, concat_axis=0, tiled=True)]
    ppermute x0 -> x15, waiting for transfers between devices: none -> 14.2 us  [exchange_in_pairs(): part = lax.ppermute(part, axis, [(d, d ^ mask) for d in range(ways)])]
    all_to_all x1 -> x0, starting transfers between devices: 6.01 us -> none  [regroup_rows(): lax.all_to_all(outgoing, 'wide', split_axis=0, concat_axis=0, tiled=True)]
  transfers between devices with their start and end apart: 10 -> 24, of which waited for: 2 -> 10; matrix products, arithmetic and copies ran while one was open for 36% -> 36% of each run, Pallas kernels for 0% -> 0%
where the time goes in v1:
time: 431 us; the launch traced here: 426 us
  matrix products  154 us (36%)
  loops' own time  80.9 us (19%)
  local copies, waits for them, and re-layouts  66.2 us (15%)
  other arithmetic  54.3 us (13%)
  starting transfers between devices  51.2 us (12%)
  waiting for transfers between devices  18.3 us (4%)
    another operation x4, loops' own time, window_attention(): heads_out = lax.map(per_head, jnp.arange(HEADS, dtype=jnp.int32))  80.9 us
    dot_general x32, matrix products, per_head(): jnp.dot(weights, values_part, preferred_element_type=jnp.float32)  80.2 us
    dot_general x32, matrix products, per_head(): lax.dot_general(query_part, keys_part, (((1,), (1,)), ((), ())), preferre...  71 us
    reduce_sum x32, other arithmetic, per_head(): totals = jnp.sum(exponents, axis=1, keepdims=True)  41.6 us
    ppermute x15, starting transfers between devices, exchange_in_pairs(): part = lax.ppermute(part, axis, [(d, d ^ mask) for d in range(ways)])  21.4 us
    dynamic_slice x32, local copies, waits for them, and re-layouts, window_attention(): heads_out = lax.map(per_head, jnp.arange(HEADS, dtype=jnp.int32))  19 us
    dynamic_slice x32, local copies, waits for them, and re-layouts, per_head(): scores = scores * factor[head_index]  19 us
    ppermute x4, starting transfers between devices, extended(): lax.ppermute(lax.slice_in_dim(block, block.shape[dim] - width, None, axis...  15.7 us
  transfers between devices with their start and end apart: 24, of which 10 were waited for; matrix products, arithmetic and copies ran while one was open for 36% of the time, Pallas kernels for 0%

profile of v1, /device:TPU:13, one launch (start us, length us, event | category | flops | bytes accessed | tf_op | source)
XLA Modules:
  0.0 425.9 jit_solution(10300831866252678732)
XLA Ops:
  2.6 3.8 collective-permute-start
  8.4 4.5 %collective-permute-start.1 = (s32[256]{0:T(256)S(1)}, s32[256]{0:T(256)S(1)}, u32[]{:S(2)}, u32[]{:S(2)}) collective-permute-start(s32[256]{0:T(256)S(1)} %get-tuple-element.555), channel_id=1, source_target_pairs={{0,1},{1,2},{2,3},{3,4},{4,5},{5,6},{6,7},{7,8},{8,9},{9,10},{10,1... | collective-permute-start | bytes 3080 | tf_op jit(solution)/shard_map/ppermute | solution.py:33
  14.9 4.5 %reduce-window.6 = s32[16,8,128]{2,1,0:T(8,128)S(1)} reduce-window(s32[16,8,128]{2,1,0:T(8,128)S(1)} %fusion.78, s32[]{:T(128)} %constant.279.clone.1), window={size=1x1x128 pad=0_0x0_0x127_0}, to_apply=%region_0.1 | reduce-window | flops 2080768 | bytes 131076 | tf_op jit(solution)/shard_map/reduce-window
  19.9 4.9 %scatter_custom_fusion = s32[2048]{0:T(1024)} fusion(s32[1024]{0:T(1024)S(1)} %get-tuple-element.558, s32[1024]{0:T(1024)S(1)} %get-tuple-element.557, s32[]{:T(128)} %constant.277.clone.1), kind=kCustom, calls=%fused_computation.156 | custom fusion | bytes 8196 | tf_op jit(solution)/shard_map/scatter | solution.py:122
  24.8 6.4 %all-to-all-start = ((s32[16,128,1]{1,2,0:T(1,128)}), s32[16,128,1]{1,2,0:T(1,128)}, u32[]{:S(2)}, u32[]{:S(2)}) async-start(s32[16,128,1]{1,2,0:T(1,128)} %bitcast.4), calls=%async_computation | async-start | bytes 16384 | tf_op jit(solution)/shard_map/all_to_all | solution.py:126
  31.8 3.5 collective-permute-start.20
  39.6 2.4 pad_maximum_fusion.3
  42.0 79.1 %while.52 = (s32[]{:T(128)}, bf16[8,512,32]{1,2,0:T(8,128)(2,1)S(1)}, s32[8]{0:T(128)S(1)}, bf16[512,256]{1,0:T(8,128)(2,1)S(1)}, bf16[1024,512]{1,0:T(8,128)(2,...) while((s32[]{:T(128)}, ...), condition=%wide.region_7.8_spmd.clone, body=%wide.region_4.7_spmd.clone.sunk | while | flops 76037128 | bytes 7010112 | solution.py:86
  49.4 2.5 fusion.117
  59.2 2.5 fusion.117
  69.1 2.5 fusion.117
  79.0 2.5 fusion.117
  88.9 2.5 fusion.117
  98.8 2.5 fusion.117
  108.7 2.5 fusion.117
  118.6 2.5 fusion.117
  121.2 79.5 %while.53 = (s32[]{:T(128)}, bf16[8,512,32]{1,2,0:T(8,128)(2,1)S(1)}, s32[8]{0:T(128)S(1)}, bf16[512,256]{1,0:T(8,128)(2,1)}, bf16[1024,512]{1,0:T(8,128)(2,1)},...) while((s32[]{:T(128)}, ...), condition=%wide.region_11.12_spmd.clone, body=%wide.region_8.11_spmd.clone.sunk | while | flops 76037128 | bytes 7010112 | solution.py:86
  125.0 2.3 fusion.119
  128.6 2.5 fusion.121
  134.9 2.3 fusion.119
  138.5 2.5 fusion.121
  144.8 2.3 fusion.119
  148.5 2.5 fusion.121
  154.8 2.3 fusion.119
  158.4 2.5 fusion.121
  164.7 2.3 fusion.119
  168.3 2.5 fusion.121
  174.7 2.3 fusion.119
  178.3 2.5 fusion.121
  184.6 2.3 fusion.119
  188.2 2.5 fusion.121
  194.6 2.3 fusion.119
  198.2 2.5 fusion.121
  201.6 5.5 %scatter_custom_fusion.1 = bf16[2048,256]{1,0:T(8,128)(2,1)S(1)} fusion(s32[1024]{0:T(1024)S(1)} %get-tuple-element.558, bf16[1024,256]{1,0:T(8,128)(2,1)S(1)} %copy.23, bf16[]{:T(256)} %constant.276.clone.1), kind=kCustom, calls=%fused_computation.90 | custom fusion | bytes 1048578 | tf_op jit(solution)/shard_map/scatter | solution.py:120
  220.2 2.8 collective-permute-start.12
  224.3 5.2 %collective-permute-start.14 = (bf16[128,256]{1,0:T(8,128)(2,1)S(1)}, bf16[128,256]{1,0:T(8,128)(2,1)S(1)}, u32[]{:S(2)}, u32[]{:S(2)}) collective-permute-start(bf16[128,256]{1,0:T(8,128)(2,1)S(1)} %get-tuple-element.531), channel_id=1, source_target_pairs={{0,11},{1,10},{2,9},{3,8},{4,15},{5,14},{6,13},{7,12},{8,3},{9,2},... | collective-permute-start | bytes 196616 | tf_op jit(solution)/shard_map/ppermute | solution.py:23
  237.0 3.3 collective-permute-done.17
  240.4 4.2 collective-permute-done.18
  244.6 9.4 %scatter_custom_fusion.2 = bf16[1024,256]{1,0:T(8,128)(2,1)S(1)} fusion(s32[2048]{0:T(1024)S(1)} %bitcast.112, bf16[2048,256]{1,0:T(8,128)(2,1)S(1)} %constant_dynamic-update-slice_fusion, bf16[]{:T(256)} %constant.276.clone.1), kind=kCustom, calls=%fused_computation.97 | custom fusion | bytes 524290 | tf_op jit(solution)/shard_map/scatter | solution.py:129
  255.3 3.8 collective-permute-start.19
  263.8 4.2 collective-permute-done.21
  268.0 2.9 pad_maximum_fusion.1
  270.9 74.0 %while.54 = (s32[]{:T(128)}, bf16[8,512,32]{1,2,0:T(8,128)(2,1)S(1)}, s32[8]{0:T(128)S(1)}, bf16[512,256]{1,0:T(8,128)(2,1)S(1)}, bf16[1024,512]{1,0:T(8,128)(2,...) while((s32[]{:T(128)}, ...), condition=%wide.region_19.20_spmd.clone, body=%wide.region_16.19_spmd.clone.sunk | while | flops 76037128 | bytes 7010112 | solution.py:86
  277.7 2.4 fusion.125
  286.9 2.4 fusion.125
  296.2 2.4 fusion.125
  305.5 2.4 fusion.125
  314.7 2.4 fusion.125
  324.0 2.4 fusion.125
  333.2 2.4 fusion.125
  342.5 2.4 fusion.125
  345.0 79.1 %while.55 = (s32[]{:T(128)}, bf16[8,512,32]{1,2,0:T(8,128)(2,1)S(1)}, s32[8]{0:T(128)S(1)}, bf16[512,256]{1,0:T(8,128)(2,1)}, bf16[1024,512]{1,0:T(8,128)(2,1)},...) while((s32[]{:T(128)}, ...), condition=%wide.region_23.24_spmd.clone, body=%wide.region_20.23_spmd.clone.sunk | while | flops 76037128 | bytes 7010112 | solution.py:86
  348.8 2.3 fusion.127
  352.4 2.5 fusion.129
  362.2 2.5 fusion.129
  368.6 2.3 fusion.127
  372.1 2.5 fusion.129
  382.0 2.5 fusion.129
  388.3 2.3 fusion.127
  391.9 2.5 fusion.129
  401.8 2.5 fusion.129
  408.1 2.3 fusion.127
  411.7 2.5 fusion.129
  421.6 2.5 fusion.129
  (250 shorter events, 165.5 us)
Async XLA Ops:
  0.0 8.4 %copy-start.9 = (s32[1024]{0:T(1024)S(1)}, s32[1024]{0:T(1024)}, u32[]{:S(2)}) copy-start(s32[1024]{0:T(1024)} %param.17) | copy-start | bytes 12292
  0.0 14.9 %copy-start.7 = (s32[1024]{0:T(1024)S(1)}, s32[1024]{0:T(1024)}, u32[]{:S(2)}) copy-start(s32[1024]{0:T(1024)} %param.19) | copy-start | bytes 12292
  0.0 31.2 %copy-start.10 = (s32[1024]{0:T(1024)S(1)}, s32[1024]{0:T(1024)}, u32[]{:S(2)}) copy-start(s32[1024]{0:T(1024)} %param.18) | copy-start | bytes 12292
  2.6 33.6 %copy-start = (bf16[1024,256]{1,0:T(8,128)(2,1)S(1)}, bf16[1024,256]{1,0:T(8,128)(2,1)}, u32[]{:S(2)}) copy-start(bf16[1024,256]{1,0:T(8,128)(2,1)} %param.16) | copy-start | bytes 1572868
  2.6 36.9 %collective-permute-start = (bf16[256,512]{1,0:T(8,128)(2,1)}, bf16[256,512]{1,0:T(8,128)(2,1)S(1)}, u32[]{:S(2)}, u32[]{:S(2)}) collective-permute-start(bf16[256,512]{1,0:T(8,128)(2,1)} %get-tuple-element.521), channel_id=1, source_target_pairs={{0,1},{1,2},{2,3},{3,4},{4,5},{5,6},{6,7},{7,8},{8,9},{9,10},{10,1... | collective-permute-start | bytes 786440 | tf_op jit(solution)/shard_map/ppermute | solution.py:33
  6.4 33.1 %collective-permute-start.2 = (bf16[256,512]{1,0:T(8,128)(2,1)}, bf16[256,512]{1,0:T(8,128)(2,1)}, u32[]{:S(2)}, u32[]{:S(2)}) collective-permute-start(bf16[256,512]{1,0:T(8,128)(2,1)} %get-tuple-element.522), channel_id=1, source_target_pairs={{1,0},{2,1},{3,2},{4,3},{5,4},{6,5},{7,6},{8,7},{9,8},{10,9},{11,1... | collective-permute-start | bytes 786440 | tf_op jit(solution)/shard_map/ppermute | solution.py:36
  8.4 29.2 %collective-permute-start.1 = (s32[256]{0:T(256)S(1)}, s32[256]{0:T(256)S(1)}, u32[]{:S(2)}, u32[]{:S(2)}) collective-permute-start(s32[256]{0:T(256)S(1)} %get-tuple-element.555), channel_id=1, source_target_pairs={{0,1},{1,2},{2,3},{3,4},{4,5},{5,6},{6,7},{7,8},{8,9},{9,10},{10,1... | collective-permute-start | bytes 3080 | tf_op jit(solution)/shard_map/ppermute | solution.py:33
  13.0 26.6 %collective-permute-start.3 = (s32[256]{0:T(256)S(1)}, s32[256]{0:T(256)S(1)}, u32[]{:S(2)}, u32[]{:S(2)}) collective-permute-start(s32[256]{0:T(256)S(1)} %get-tuple-element.556), channel_id=1, source_target_pairs={{1,0},{2,1},{3,2},{4,3},{5,4},{6,5},{7,6},{8,7},{9,8},{10,9},{11,1... | collective-permute-start | bytes 3080 | tf_op jit(solution)/shard_map/ppermute | solution.py:36
  24.8 183.9 %all-to-all-start = ((s32[16,128,1]{1,2,0:T(1,128)}), s32[16,128,1]{1,2,0:T(1,128)}, u32[]{:S(2)}, u32[]{:S(2)}) async-start(s32[16,128,1]{1,2,0:T(1,128)} %bitcast.4), calls=%async_computation | async-start | bytes 16384 | tf_op jit(solution)/shard_map/all_to_all | solution.py:126
  31.2 5.3 %copy-start.5 = (s32[1024]{0:T(1024)}, s32[1024]{0:T(1024)S(1)}, u32[]{:S(2)}) copy-start(s32[1024]{0:T(1024)S(1)} %broadcast_add_fusion.1) | copy-start | bytes 12292
  31.8 4.7 %copy-start.11 = (f32[2,256]{1,0:T(2,128)S(1)}, f32[2,256]{1,0:T(2,128)}, u32[]{:S(2)}) copy-start(f32[2,256]{1,0:T(2,128)} %param.22) | copy-start | bytes 6148
  31.8 5.3 %copy-start.12 = (f32[2,8]{1,0:T(2,128)S(1)}, f32[2,8]{1,0:T(2,128)}, u32[]{:S(2)}) copy-start(f32[2,8]{1,0:T(2,128)} %param.23) | copy-start | bytes 196
  31.8 229.3 %collective-permute-start.20 = (s32[256]{0:T(256)}, s32[256]{0:T(256)}, u32[]{:S(2)}, u32[]{:S(2)}) collective-permute-start(s32[256]{0:T(256)} %get-tuple-element.549), channel_id=1, source_target_pairs={{0,1},{1,2},{2,3},{3,4},{4,5},{5,6},{6,7},{7,8},{8,9},{9,10},{10,1... | collective-permute-start | bytes 3080 | tf_op jit(solution)/shard_map/ppermute | solution.py:33
  36.4 5.6 %copy-start.4 = (bf16[512,256]{1,0:T(8,128)(2,1)S(1)}, bf16[512,256]{1,0:T(8,128)(2,1)}, u32[]{:S(2)}) copy-start(bf16[512,256]{1,0:T(8,128)(2,1)} %get-tuple-element.829) | copy-start | bytes 786436
  37.6 223.5 %collective-permute-start.22 = (s32[256]{0:T(256)}, s32[256]{0:T(256)}, u32[]{:S(2)}, u32[]{:S(2)}) collective-permute-start(s32[256]{0:T(256)} %get-tuple-element.550), channel_id=1, source_target_pairs={{1,0},{2,1},{3,2},{4,3},{5,4},{6,5},{7,6},{8,7},{9,8},{10,9},{11,1... | collective-permute-start | bytes 3080 | tf_op jit(solution)/shard_map/ppermute | solution.py:36
  121.2 79.6 %copy-start.2 = (bf16[2,256,256]{2,1,0:T(8,128)(2,1)S(1)}, bf16[2,256,256]{2,1,0:T(8,128)(2,1)}, u32[]{:S(2)}) copy-start(bf16[2,256,256]{2,1,0:T(8,128)(2,1)} %param.21) | copy-start | bytes 786436
  207.2 46.8 %copy-start.1 = (bf16[2,256,768]{2,1,0:T(8,128)(2,1)S(1)}, bf16[2,256,768]{2,1,0:T(8,128)(2,1)}, u32[]{:S(2)}) copy-start(bf16[2,256,768]{2,1,0:T(8,128)(2,1)} %param.20) | copy-start | bytes 2359300
  208.0 3.1 collective-permute-start.4
  209.4 3.9 collective-permute-start.5
  210.6 4.6 %collective-permute-start.6 = (bf16[128,256]{1,0:T(8,128)(2,1)}, bf16[128,256]{1,0:T(8,128)(2,1)S(1)}, u32[]{:S(2)}, u32[]{:S(2)}) collective-permute-start(bf16[128,256]{1,0:T(8,128)(2,1)} %get-tuple-element.539), channel_id=1, source_target_pairs={{0,3},{1,2},{2,1},{3,0},{4,7},{5,6},{6,5},{7,4},{8,11},{9,10},{10,... | collective-permute-start | bytes 196616 | tf_op jit(solution)/shard_map/ppermute | solution.py:23
  211.1 5.9 %collective-permute-start.7 = (bf16[128,256]{1,0:T(8,128)(2,1)}, bf16[128,256]{1,0:T(8,128)(2,1)S(1)}, u32[]{:S(2)}, u32[]{:S(2)}) collective-permute-start(bf16[128,256]{1,0:T(8,128)(2,1)} %get-tuple-element.538), channel_id=1, source_target_pairs={{0,4},{1,5},{2,6},{3,7},{4,0},{5,1},{6,2},{7,3},{8,12},{9,13},{10,... | collective-permute-start | bytes 196616 | tf_op jit(solution)/shard_map/ppermute | solution.py:23
  213.3 4.7 %collective-permute-start.8 = (bf16[128,256]{1,0:T(8,128)(2,1)}, bf16[128,256]{1,0:T(8,128)(2,1)S(1)}, u32[]{:S(2)}, u32[]{:S(2)}) collective-permute-start(bf16[128,256]{1,0:T(8,128)(2,1)} %get-tuple-element.537), channel_id=1, source_target_pairs={{0,5},{1,4},{2,7},{3,6},{4,1},{5,0},{6,3},{7,2},{8,13},{9,12},{10,... | collective-permute-start | bytes 196616 | tf_op jit(solution)/shard_map/ppermute | solution.py:23
  215.2 5.1 %collective-permute-start.9 = (bf16[128,256]{1,0:T(8,128)(2,1)S(1)}, bf16[128,256]{1,0:T(8,128)(2,1)S(1)}, u32[]{:S(2)}, u32[]{:S(2)}) collective-permute-start(bf16[128,256]{1,0:T(8,128)(2,1)S(1)} %get-tuple-element.536), channel_id=1, source_target_pairs={{0,6},{1,7},{2,4},{3,5},{4,2},{5,3},{6,0},{7,1},{8,14},{9,15},{10,... | collective-permute-start | bytes 196616 | tf_op jit(solution)/shard_map/ppermute | solution.py:23
  216.9 6.1 %collective-permute-start.10 = (bf16[128,256]{1,0:T(8,128)(2,1)S(1)}, bf16[128,256]{1,0:T(8,128)(2,1)S(1)}, u32[]{:S(2)}, u32[]{:S(2)}) collective-permute-start(bf16[128,256]{1,0:T(8,128)(2,1)S(1)} %get-tuple-element.535), channel_id=1, source_target_pairs={{0,7},{1,6},{2,5},{3,4},{4,3},{5,2},{6,1},{7,0},{8,15},{9,14},{10,... | collective-permute-start | bytes 196616 | tf_op jit(solution)/shard_map/ppermute | solution.py:23
  217.9 6.3 %collective-permute-start.11 = (bf16[128,256]{1,0:T(8,128)(2,1)S(1)}, bf16[128,256]{1,0:T(8,128)(2,1)S(1)}, u32[]{:S(2)}, u32[]{:S(2)}) collective-permute-start(bf16[128,256]{1,0:T(8,128)(2,1)S(1)} %get-tuple-element.534), channel_id=1, source_target_pairs={{0,8},{1,9},{2,10},{3,11},{4,12},{5,13},{6,14},{7,15},{8,0},{9,1},... | collective-permute-start | bytes 196616 | tf_op jit(solution)/shard_map/ppermute | solution.py:23
  220.2 9.2 %collective-permute-start.12 = (bf16[128,256]{1,0:T(8,128)(2,1)S(1)}, bf16[128,256]{1,0:T(8,128)(2,1)S(1)}, u32[]{:S(2)}, u32[]{:S(2)}) collective-permute-start(bf16[128,256]{1,0:T(8,128)(2,1)S(1)} %get-tuple-element.533), channel_id=1, source_target_pairs={{0,9},{1,8},{2,11},{3,10},{4,13},{5,12},{6,15},{7,14},{8,1},{9,0},... | collective-permute-start | bytes 196616 | tf_op jit(solution)/shard_map/ppermute | solution.py:23
  223.0 7.5 %collective-permute-start.13 = (bf16[128,256]{1,0:T(8,128)(2,1)S(1)}, bf16[128,256]{1,0:T(8,128)(2,1)S(1)}, u32[]{:S(2)}, u32[]{:S(2)}) collective-permute-start(bf16[128,256]{1,0:T(8,128)(2,1)S(1)} %get-tuple-element.532), channel_id=1, source_target_pairs={{0,10},{1,11},{2,8},{3,9},{4,14},{5,15},{6,12},{7,13},{8,2},{9,3},... | collective-permute-start | bytes 196616 | tf_op jit(solution)/shard_map/ppermute | solution.py:23
  224.3 7.7 %collective-permute-start.14 = (bf16[128,256]{1,0:T(8,128)(2,1)S(1)}, bf16[128,256]{1,0:T(8,128)(2,1)S(1)}, u32[]{:S(2)}, u32[]{:S(2)}) collective-permute-start(bf16[128,256]{1,0:T(8,128)(2,1)S(1)} %get-tuple-element.531), channel_id=1, source_target_pairs={{0,11},{1,10},{2,9},{3,8},{4,15},{5,14},{6,13},{7,12},{8,3},{9,2},... | collective-permute-start | bytes 196616 | tf_op jit(solution)/shard_map/ppermute | solution.py:23
  229.5 6.0 %collective-permute-start.15 = (bf16[128,256]{1,0:T(8,128)(2,1)S(1)}, bf16[128,256]{1,0:T(8,128)(2,1)S(1)}, u32[]{:S(2)}, u32[]{:S(2)}) collective-permute-start(bf16[128,256]{1,0:T(8,128)(2,1)S(1)} %get-tuple-element.530), channel_id=1, source_target_pairs={{0,12},{1,13},{2,14},{3,15},{4,8},{5,9},{6,10},{7,11},{8,4},{9,5},... | collective-permute-start | bytes 196616 | tf_op jit(solution)/shard_map/ppermute | solution.py:23
  230.5 6.4 %collective-permute-start.16 = (bf16[128,256]{1,0:T(8,128)(2,1)S(1)}, bf16[128,256]{1,0:T(8,128)(2,1)S(1)}, u32[]{:S(2)}, u32[]{:S(2)}) collective-permute-start(bf16[128,256]{1,0:T(8,128)(2,1)S(1)} %get-tuple-element.529), channel_id=1, source_target_pairs={{0,13},{1,12},{2,15},{3,14},{4,9},{5,8},{6,11},{7,10},{8,5},{9,4},... | collective-permute-start | bytes 196616 | tf_op jit(solution)/shard_map/ppermute | solution.py:23
  231.9 8.4 %collective-permute-start.17 = (bf16[128,256]{1,0:T(8,128)(2,1)S(1)}, bf16[128,256]{1,0:T(8,128)(2,1)S(1)}, u32[]{:S(2)}, u32[]{:S(2)}) collective-permute-start(bf16[128,256]{1,0:T(8,128)(2,1)S(1)} %get-tuple-element.528), channel_id=1, source_target_pairs={{0,14},{1,15},{2,12},{3,13},{4,10},{5,11},{6,8},{7,9},{8,6},{9,7},... | collective-permute-start | bytes 196616 | tf_op jit(solution)/shard_map/ppermute | solution.py:23
  235.5 9.1 %collective-permute-start.18 = (bf16[128,256]{1,0:T(8,128)(2,1)S(1)}, bf16[128,256]{1,0:T(8,128)(2,1)S(1)}, u32[]{:S(2)}, u32[]{:S(2)}) collective-permute-start(bf16[128,256]{1,0:T(8,128)(2,1)S(1)} %get-tuple-element.527), channel_id=1, source_target_pairs={{0,15},{1,14},{2,13},{3,12},{4,11},{5,10},{6,9},{7,8},{8,7},{9,6},... | collective-permute-start | bytes 196616 | tf_op jit(solution)/shard_map/ppermute | solution.py:23
  240.3 20.8 %copy-start.6 = (s32[1024]{0:T(1024)S(1)}, s32[1024]{0:T(1024)}, u32[]{:S(2)}) copy-start(s32[1024]{0:T(1024)} %copy-done.5) | copy-start | bytes 12292
  255.3 8.5 %collective-permute-start.19 = (bf16[256,512]{1,0:T(8,128)(2,1)}, bf16[256,512]{1,0:T(8,128)(2,1)S(1)}, u32[]{:S(2)}, u32[]{:S(2)}) collective-permute-start(bf16[256,512]{1,0:T(8,128)(2,1)} %get-tuple-element.517), channel_id=1, source_target_pairs={{0,1},{1,2},{2,3},{3,4},{4,5},{5,6},{6,7},{7,8},{8,9},{9,10},{10,1... | collective-permute-start | bytes 786440 | tf_op jit(solution)/shard_map/ppermute | solution.py:33
  259.2 8.8 %collective-permute-start.21 = (bf16[256,512]{1,0:T(8,128)(2,1)}, bf16[256,512]{1,0:T(8,128)(2,1)S(1)}, u32[]{:S(2)}, u32[]{:S(2)}) collective-permute-start(bf16[256,512]{1,0:T(8,128)(2,1)} %get-tuple-element.518), channel_id=1, source_target_pairs={{1,0},{2,1},{3,2},{4,3},{5,4},{6,5},{7,6},{8,7},{9,8},{10,9},{11,1... | collective-permute-start | bytes 786440 | tf_op jit(solution)/shard_map/ppermute | solution.py:36
  263.8 7.1 %copy-start.13 = (f32[8]{0:T(128)S(1)}, f32[8]{0:T(128)}, u32[]{:S(2)}) copy-start(f32[8]{0:T(128)} %get-tuple-element.921) | copy-start | bytes 100
  345.0 79.1 %copy-start.3 = (bf16[2,256,256]{2,1,0:T(8,128)(2,1)S(1)}, bf16[2,256,256]{2,1,0:T(8,128)(2,1)}, u32[]{:S(2)}) copy-start(bf16[2,256,256]{2,1,0:T(8,128)(2,1)} %param.21) | copy-start | bytes 786436
  424.1 0.6 copy-start.8
